TPU v7x, 512 devices: a whole 4x4x16 slice. The times are simulated.
512 devices in a mesh: cp: 64 (over y, x, z_lo), sp: 8 (over z_hi, core).
Axes of the slice: x: 4, y: 4, z: 16 (z_hi: 4, z_lo: 4; z = z_hi * 4 + z_lo), core: 2. Of those that a mesh axis runs over, the one named last changes fastest.
Arguments:
- queries: bfloat16 [16384, 2048], P('cp', 'sp'), may hold values from -22 to 22
- keys: bfloat16 [16384, 128], P(('cp', 'sp')), may hold values from -5 to 5
- values: bfloat16 [16384, 128], P(('cp', 'sp')), may hold values from -6 to 6
- doc_ids: int32 [128], replicated, may hold values from 0 to 31, never falling along the last dimension, each value on 1 to 32 neighbouring positions
- span_order: int32 [64], replicated, may hold values from 0 to 63, each once
Outputs:
- attended: bfloat16 [16384, 2048], P('cp', 'sp')
Inputs may be any that keep to these rules, and one draw needn't show every extreme that they name: doc_ids never falls; each document covers 1 to 32 consecutive blocks, and one covers exactly 32. Index i of cp holds span span_order[i] of the sequence; each span once.
All inputs are finite; a program needn't handle non-finite values.
Results may differ from a plain program's by a relative error of at most 0.0036.
Values may be sent and summed in bfloat16 or wider, within the bound.
A program may use at most 64 MiB of HBM per device.

v0:
```python
import math
import jax
import jax.numpy as jnp
from jax import lax
from jax.sharding import PartitionSpec as P

HD = 128
SPAN = 256
BLK = 128
NEGATIVE = -1e30


def true_position(row_ids, span_order):
    span_index = row_ids // SPAN
    lookup = jnp.arange(span_order.shape[0], dtype=jnp.int32)
    placed = jnp.sum(
        jnp.where(span_index[:, None] == lookup[None, :], span_order[None, :], 0), axis=1
    )
    return placed * SPAN + row_ids % SPAN


def doc_lookup(position, doc_ids):
    block_index = position // BLK
    lookup = jnp.arange(doc_ids.shape[0], dtype=jnp.int32)
    return jnp.sum(jnp.where(block_index[:, None] == lookup[None, :], doc_ids[None, :], 0), axis=1)


def make_folder(query_block, query_pos, query_doc, span_order, doc_ids):
    score_scale = 1.0 / math.sqrt(query_block.shape[2])

    def fold_piece(carried, piece, start):
        key_piece, value_piece = piece
        piece_rows = key_piece.shape[0]
        tile_rows = math.gcd(piece_rows, SPAN)
        tile_count = piece_rows // tile_rows
        key_tiles = key_piece.reshape(tile_count, tile_rows, key_piece.shape[1])
        value_tiles = value_piece.reshape(tile_count, tile_rows, value_piece.shape[1])

        def tile_step(state_now, tile_inputs):
            key_tile, value_tile, tile_index = tile_inputs
            row_ids = tile_index * tile_rows + jnp.arange(tile_rows, dtype=jnp.int32)
            key_pos = true_position(row_ids, span_order)
            key_doc = doc_lookup(key_pos, doc_ids)
            allowed = (key_pos[None, :] <= query_pos[:, None]) & (
                key_doc[None, :] == query_doc[:, None]
            )
            run_max, run_total, run_accum = state_now
            scores = (
                jnp.einsum("rhd,kd->hrk", query_block, key_tile, preferred_element_type=jnp.float32)
                * score_scale
            )
            masked = jnp.where(allowed[None], scores, NEGATIVE)
            new_max = jnp.maximum(run_max, jnp.max(masked, axis=2))
            rescale = jnp.exp(run_max - new_max)
            weights = jnp.where(allowed[None], jnp.exp(masked - new_max[:, :, None]), 0.0)
            new_total = run_total * rescale + jnp.sum(weights, axis=2)
            product = jnp.einsum(
                "hrk,kd->rhd",
                weights.astype(jnp.bfloat16),
                value_tile,
                preferred_element_type=jnp.float32,
            )
            new_accum = run_accum * jnp.transpose(rescale)[:, :, None] + product
            result = (new_max, new_total, new_accum)
            return (result, None)

        tile_ids = jnp.arange(tile_count, dtype=jnp.int32)
        carried, unused = lax.scan(tile_step, carried, (key_tiles, value_tiles, tile_ids))
        return carried

    return fold_piece


def shards(queries, keys, values, doc_ids, span_order):
    cp_index = lax.axis_index("cp")
    query_ids = cp_index * SPAN + jnp.arange(queries.shape[0], dtype=jnp.int32)
    query_count = queries.shape[0]
    head_count = queries.shape[1] // HD
    query_block = queries.reshape(query_count, head_count, HD)
    query_pos = true_position(query_ids, span_order)
    query_doc = doc_lookup(query_pos, doc_ids)
    folder = make_folder(query_block, query_pos, query_doc, span_order, doc_ids)
    initial = (
        jnp.full((head_count, query_count), NEGATIVE, jnp.float32),
        jnp.zeros((head_count, query_count), jnp.float32),
        jnp.zeros((query_count, head_count, HD), jnp.float32),
    )
    group_keys, group_values = (
        lax.all_gather(keys, "sp", axis=0, tiled=True),
        lax.all_gather(values, "sp", axis=0, tiled=True),
    )
    final = folder(
        initial,
        (
            lax.all_gather(group_keys, "cp", axis=0, tiled=True),
            lax.all_gather(group_values, "cp", axis=0, tiled=True),
        ),
        jnp.int32(0),
    )
    run_max, run_total, run_accum = final
    attended = (run_accum / jnp.transpose(run_total)[:, :, None]).astype(jnp.bfloat16)
    attended = attended.reshape(query_count, head_count * HD)
    return attended


def solution(mesh):
    in_specs = (P("cp", "sp"), P(("cp", "sp"), None), P(("cp", "sp"), None), P(), P())
    out_specs = P("cp", "sp")
    return jax.shard_map(shards, mesh=mesh, in_specs=in_specs, out_specs=out_specs, check_vma=False)
```

profile of v0, /device:TPU:94, one launch (start us, length us, event | category | flops | bytes accessed | tf_op | source)
XLA Modules:
  0.0 1104.7 jit_solution(16146311559544574172)
XLA Ops:
  6.5 26.0 %all_gather.12 = bf16[256,128]{1,0:T(8,128)(2,1)} all-gather(bf16[32,128]{1,0:T(8,128)(2,1)} %param.8), channel_id=1, replica_groups=mesh['cp'=64,'sp'=8] {'sp'}, dimensions={0}, use_global_device_ids=true | all-gather | bytes 73728 | tf_op jit(solution)/shard_map/all_gather | solution.py:89
  32.6 19.5 %all_gather.14 = bf16[256,128]{1,0:T(8,128)(2,1)} all-gather(bf16[32,128]{1,0:T(8,128)(2,1)} %param.9), channel_id=1, replica_groups=mesh['cp'=64,'sp'=8] {'sp'}, dimensions={0}, use_global_device_ids=true | all-gather | bytes 73728 | tf_op jit(solution)/shard_map/all_gather | solution.py:90
  55.0 337.2 %all-gather.3.cloned.1.call-done = bf16[16384,128]{1,0:T(8,128)(2,1)} async-done(((bf16[256,128]{1,0:T(8,128)(2,1)}), bf16[16384,128]{1,0:T(8,128)(2,1)}) %all-gather.3.cloned.1.call-update) | async-done | bytes 4194320 | tf_op jit(solution)/shard_map/all_gather | solution.py:95
  392.1 362.4 %all-gather.5.cloned.1.call-done = bf16[16384,128]{1,0:T(8,128)(2,1)} async-done(((bf16[256,128]{1,0:T(8,128)(2,1)}), bf16[16384,128]{1,0:T(8,128)(2,1)}) %all-gather.5.cloned.1.call-update) | async-done | bytes 4194320 | tf_op jit(solution)/shard_map/all_gather | solution.py:96
  754.5 342.6 %while.18 = (s32[]{:T(128)}, f32[2,256]{1,0:T(2,128)S(1)}, f32[2,256]{1,0:T(2,128)S(1)}, f32[256,2,128]{0,2,1:T(8,128)S(1)}, s32[64]{0:T(128)S(1)}, /*index=5*/s...) while((s32[]{:T(128)}, f32[2,256]{1,0:T(2,128)S(1)}, ...), condition=%wide.region_7.8_spmd.clone, body=%wide.region_2.7_spmd.clone.sunk | while | flops 68843264 | bytes 2668473 | solution.py:68
  758.5 1.1 fusion.43
  763.9 1.1 fusion.43
  769.2 1.1 fusion.43
  774.6 1.1 fusion.43
  779.9 1.1 fusion.43
  785.3 1.1 fusion.43
  790.6 1.1 fusion.43
  796.0 1.1 fusion.43
  801.4 1.1 fusion.43
  806.7 1.1 fusion.43
  812.1 1.1 fusion.43
  817.4 1.1 fusion.43
  822.8 1.1 fusion.43
  828.1 1.1 fusion.43
  833.5 1.1 fusion.43
  838.8 1.1 fusion.43
  844.2 1.1 fusion.43
  849.5 1.1 fusion.43
  854.9 1.1 fusion.43
  860.2 1.1 fusion.43
  865.6 1.1 fusion.43
  870.9 1.1 fusion.43
  876.3 1.1 fusion.43
  881.7 1.1 fusion.43
  887.0 1.1 fusion.43
  892.4 1.1 fusion.43
  897.7 1.1 fusion.43
  (757 shorter events, 274.2 us)
Async XLA Ops:
  6.5 385.6 %all-gather.3.cloned.1.call-start = ((), (), s32[]{:S(2)}) async-start(), calls=%async_computation | async-start | bytes 4259840 | tf_op jit(solution)/shard_map/all_gather | solution.py:95
  32.6 721.9 %all-gather.5.cloned.1.call-start = ((), (), s32[]{:S(2)}) async-start(), calls=%async_computation.1 | async-start | bytes 4259840 | tf_op jit(solution)/shard_map/all_gather | solution.py:96
Sparse Core Ops, SparseCore 0:
  32.7 359.3 all-gather.2
  394.2 360.2 all-gather.4
where the time goes:
time: 1110 us; the launch traced here: 1100 us
  waiting for transfers between devices  700 us (63%)
  matrix products  143 us (13%)
  other arithmetic  124 us (11%)
  blocking collectives  45.5 us (4%)
  loops' own time  40.9 us (4%)
  local copies, waits for them, and re-layouts  37.8 us (3%)
  between operations  13.5 us (1%)
    all_gather x1, waiting for transfers between devices, shards(): lax.all_gather(group_values, 'cp', axis=0, tiled=True)  362 us
    all_gather x1, waiting for transfers between devices, shards(): lax.all_gather(group_keys, 'cp', axis=0, tiled=True)  337 us
    dot_general x64, matrix products, tile_step(): jnp.einsum('hrk,kd->rhd', weights.astype(jnp.bfloat16), value_tile, prefe...  73.6 us
    dot_general x64, matrix products, tile_step(): jnp.einsum('rhd,kd->hrk', query_block, key_tile, preferred_element_type=j...  69.8 us
    reduce_sum x65, other arithmetic, doc_lookup(): jnp.sum(jnp.where(block_index[:, None] == lookup[None, :], doc_ids[None,...  54.1 us
    reduce_sum x65, other arithmetic, true_position(): jnp.sum(jnp.where(span_index[:, None] == lookup[None, :], span_order[None...  48.6 us
    another operation x1, loops' own time, fold_piece(): lax.scan(tile_step, carried, (key_tiles, value_tiles, tile_ids))  40.9 us
    dynamic_slice x64, local copies, waits for them, and re-layouts, fold_piece(): lax.scan(tile_step, carried, (key_tiles, value_tiles, tile_ids))  35.8 us
  transfers between devices with their start and end apart: 2, of which 2 were waited for; matrix products, arithmetic and copies ran while one was open for 0% of the time, Pallas kernels for 0%

commit v1 on v0

--- a/solution.py
+++ b/solution.py
@@ -1,3 +1,4 @@
+import functools
 import math
 import jax
 import jax.numpy as jnp
@@ -8,6 +9,15 @@
 SPAN = 256
 BLK = 128
 NEGATIVE = -1e30
+
+
+def _review_tokens(view, out_dim):
+    x_next = jnp.stack([view for _ in range(lax.axis_size("cp"))])
+    local_out = lax.all_to_all(x_next, "cp", 0, 0)
+    return jnp.concatenate(local_out, out_dim)
+
+
+match_targets_on_mesh = functools.partial(_review_tokens, out_dim=0)
 
 
 def true_position(row_ids, span_order):
@@ -91,10 +101,7 @@
     )
     final = folder(
         initial,
-        (
-            lax.all_gather(group_keys, "cp", axis=0, tiled=True),
-            lax.all_gather(group_values, "cp", axis=0, tiled=True),
-        ),
+        (lax.all_gather(group_keys, "cp", axis=0, tiled=True), match_targets_on_mesh(group_values)),
         jnp.int32(0),
     )
     run_max, run_total, run_accum = final

time: 1110 us -> 784 us (0.71)
  waiting for transfers between devices: 700 us -> 361 us
  other arithmetic: 124 us -> 39.1 us
  blocking collectives: 45.5 us -> 129 us
    all_gather x1 -> x0, waiting for transfers between devices: 362 us -> none  [shards(): lax.all_gather(group_values, 'cp', axis=0, tiled=True)]
    all_gather x1, blocking collectives: 26 us -> 104 us  [shards(): lax.all_gather(keys, 'sp', axis=0, tiled=True)]
    reduce_sum x65, other arithmetic: 48.6 us -> 6.09 us  [true_position(): jnp.sum(jnp.where(span_index[:, None] == lookup[None, :], span_order[None...]
    reduce_sum x65, other arithmetic: 54.1 us -> 11.8 us  [doc_lookup(): jnp.sum(jnp.where(block_index[:, None] == lookup[None, :], doc_ids[None,...]
    all_gather x1, waiting for transfers between devices: 337 us -> 361 us  [shards(): lax.all_gather(group_keys, 'cp', axis=0, tiled=True)]
  transfers between devices with their start and end apart: 2 -> 2, of which waited for: 2 -> 1; matrix products, arithmetic and copies ran while one was open for 0% -> 0% of each run, Pallas kernels for 0% -> 0%
where the time goes in v1:
time: 784 us; the launch traced here: 777 us
  waiting for transfers between devices  361 us (46%)
  matrix products  143 us (18%)
  blocking collectives  129 us (16%)
  loops' own time  40.9 us (5%)
  local copies, waits for them, and re-layouts  39.5 us (5%)
  other arithmetic  39.1 us (5%)
  between operations  13.5 us (2%)
  starting transfers between devices  10.6 us (1%)
    all_gather x1, waiting for transfers between devices, shards(): lax.all_gather(group_keys, 'cp', axis=0, tiled=True)  361 us
    all_gather x1, blocking collectives, shards(): lax.all_gather(keys, 'sp', axis=0, tiled=True)  104 us
    dot_general x64, matrix products, tile_step(): jnp.einsum('hrk,kd->rhd', weights.astype(jnp.bfloat16), value_tile, prefe...  73.5 us
    dot_general x64, matrix products, tile_step(): jnp.einsum('rhd,kd->hrk', query_block, key_tile, preferred_element_type=j...  69.7 us
    another operation x1, loops' own time, fold_piece(): lax.scan(tile_step, carried, (key_tiles, value_tiles, tile_ids))  40.9 us
    dynamic_slice x64, local copies, waits for them, and re-layouts, fold_piece(): lax.scan(tile_step, carried, (key_tiles, value_tiles, tile_ids))  35.8 us
    all_gather x1, blocking collectives, shards(): lax.all_gather(values, 'sp', axis=0, tiled=True)  25 us
  transfers between devices with their start and end apart: 2, of which 1 were waited for; matrix products, arithmetic and copies ran while one was open for 0% of the time, Pallas kernels for 0%

profile of v1, /device:TPU:94, one launch (start us, length us, event | category | flops | bytes accessed | tf_op | source)
XLA Modules:
  0.0 777.1 jit_solution(10586866994038913129)
XLA Ops:
  6.5 25.0 %all_gather.11 = bf16[256,128]{1,0:T(8,128)(2,1)S(1)} all-gather(bf16[32,128]{1,0:T(8,128)(2,1)} %param.9), channel_id=1, replica_groups=mesh['cp'=64,'sp'=8] {'sp'}, dimensions={0}, use_global_device_ids=true | all-gather | bytes 73728 | tf_op jit(solution)/shard_map/all_gather | solution.py:100
  31.6 2.5 stack.2
  34.1 10.5 %all-to-all-start = ((bf16[64,256,128]{1,2,0:T(8,128)(2,1)}), bf16[64,256,128]{1,2,0:T(8,128)(2,1)}, u32[]{:S(2)}, u32[]{:S(2)}) async-start(bf16[64,256,128]{1,2,0:T(8,128)(2,1)} %stack.2), calls=%async_computation | async-start | bytes 8388608 | tf_op jit(solution)/shard_map/all_to_all | solution.py:16
  44.7 104.3 %all_gather.9 = bf16[256,128]{1,0:T(8,128)(2,1)} all-gather(bf16[32,128]{1,0:T(8,128)(2,1)S(1)} %copy-done.3), channel_id=1, replica_groups=mesh['cp'=64,'sp'=8] {'sp'}, dimensions={0}, use_global_device_ids=true | all-gather | bytes 73728 | tf_op jit(solution)/shard_map/all_gather | solution.py:99
  149.6 361.0 %all-gather.2.cloned.1.call-done = bf16[16384,128]{1,0:T(8,128)(2,1)} async-done(((bf16[256,128]{1,0:T(8,128)(2,1)}), bf16[16384,128]{1,0:T(8,128)(2,1)}) %all-gather.2.cloned.1.call-update) | async-done | bytes 4194320 | tf_op jit(solution)/shard_map/all_gather | solution.py:104
  510.6 258.8 %while.18 = (s32[]{:T(128)}, f32[2,256]{1,0:T(2,128)S(1)}, f32[2,256]{1,0:T(2,128)S(1)}, f32[256,2,128]{0,2,1:T(8,128)S(1)}, s32[64]{0:T(128)S(1)}, /*index=5*/s...) while((s32[]{:T(128)}, f32[2,256]{1,0:T(2,128)S(1)}, ...), condition=%wide.region_7.8_spmd.clone, body=%wide.region_2.7_spmd.clone.sunk | while | flops 68843264 | bytes 2668473 | solution.py:78
  517.4 1.1 fusion.43
  525.5 1.1 fusion.43
  533.5 1.1 fusion.43
  541.6 1.1 fusion.43
  549.7 1.1 fusion.43
  557.8 1.1 fusion.43
  561.9 1.1 fusion.43
  578.0 1.1 fusion.43
  586.1 1.1 fusion.43
  594.2 1.1 fusion.43
  602.3 1.1 fusion.43
  618.5 1.1 fusion.43
  634.6 1.1 fusion.43
  663.0 1.1 fusion.43
  671.0 1.1 fusion.43
  679.1 1.1 fusion.43
  687.2 1.1 fusion.43
  695.3 1.1 fusion.43
  703.4 1.1 fusion.43
  707.4 1.1 fusion.43
  711.5 1.1 fusion.43
  719.6 1.1 fusion.43
  723.6 1.1 fusion.43
  739.8 1.1 fusion.43
  747.9 1.1 fusion.43
  756.0 1.1 fusion.43
  (766 shorter events, 189.5 us)
Async XLA Ops:
  34.1 10.6 %copy-start.3 = (bf16[32,128]{1,0:T(8,128)(2,1)S(1)}, bf16[32,128]{1,0:T(8,128)(2,1)}, u32[]{:S(2)}) copy-start(bf16[32,128]{1,0:T(8,128)(2,1)} %param.8) | copy-start | bytes 24580
  34.1 114.9 %copy-start = (bf16[256,256]{1,0:T(8,128)(2,1)S(1)}, bf16[256,256]{1,0:T(8,128)(2,1)}, u32[]{:S(2)}) copy-start(bf16[256,256]{1,0:T(8,128)(2,1)} %param.7) | copy-start | bytes 393220
  34.1 115.2 %copy-start.1 = (s32[64]{0:T(128)S(1)}, s32[64]{0:T(128)}, u32[]{:S(2)}) copy-start(s32[64]{0:T(128)} %param.11) | copy-start | bytes 772
  34.1 115.3 %copy-start.2 = (s32[128]{0:T(128)S(1)}, s32[128]{0:T(128)}, u32[]{:S(2)}) copy-start(s32[128]{0:T(128)} %param.10) | copy-start | bytes 1540
  34.1 476.5 %all-to-all-start = ((bf16[64,256,128]{1,2,0:T(8,128)(2,1)}), bf16[64,256,128]{1,2,0:T(8,128)(2,1)}, u32[]{:S(2)}, u32[]{:S(2)}) async-start(bf16[64,256,128]{1,2,0:T(8,128)(2,1)} %stack.2), calls=%async_computation | async-start | bytes 8388608 | tf_op jit(solution)/shard_map/all_to_all | solution.py:16
  44.7 465.9 %all-gather.2.cloned.1.call-start = ((), (), s32[]{:S(2)}) async-start(), calls=%async_computation.1 | async-start | bytes 4259840 | tf_op jit(solution)/shard_map/all_gather | solution.py:104
Sparse Core Ops, SparseCore 0:
  149.1 361.4 all-gather.1
